TPU v7x, 256 devices: a whole 4x4x8 slice. The times are simulated.
256 devices in a mesh: blk: 16 (over x_lo, y, core), head: 16 (over x_hi, z).
Axes of the slice: x: 4 (x_hi: 2, x_lo: 2; x = x_hi * 2 + x_lo), y: 4, z: 8, core: 2. Of those that a mesh axis runs over, the one named last changes fastest.
Arguments:
- queries: bfloat16 [32768, 2048], P(('blk', 'head')), may hold values from -6 to 6
- key_rows: bfloat16 [32768, 2048], P(('blk', 'head')), may hold values from -6 to 6
- value_rows: bfloat16 [32768, 2048], P(('blk', 'head')), may hold values from -6 to 6
- w_out: bfloat16 [2048, 2048], P('head'), may hold values from -0.125 to 0.125
- first_key: int32 [32768], P('blk'), may hold values from 0 to 32765, as said below
Outputs:
- mixed: bfloat16 [32768, 2048], P(('blk', 'head'))
Inputs may be any that keep to these rules, and one draw needn't show every extreme that they name: first_key[i] <= max(i - 1, 0) and first_key[i] >= i - 2048; the last bin of each aligned block of 2048 bins has first_key exactly i - 2048 where that is not negative; the next-to-last bin of the sequence has first_key exactly 32765.
All inputs are finite; a program needn't handle non-finite values.
Results may differ from a plain program's by a relative error of at most 0.0055.
Values may be sent and summed in bfloat16 or wider, within the bound.
No kernel may reach another device: no remote copies, remote signals or barrier semaphores. Data moves between devices by JAX's collectives and lax.ppermute only.
A program may use at most 64 MiB of HBM per device.

v0:
```python
import jax
import jax.numpy as jnp
from jax import lax
from jax.sharding import PartitionSpec as P

HEAD_DIM = 64


def from_behind(x, axis, by):
    devices = lax.axis_size(axis)
    pairs = [(i, i + by) for i in range(devices) if 0 <= i + by < devices]
    return lax.ppermute(x, axis, pairs)


def attend(query_tile, key_tile, value_tile, lowest, query_pos, key_pos):
    scores = lax.dot_general(
        query_tile, key_tile, (((1,), (1,)), ((), ())), preferred_element_type=jnp.float32
    )
    scores = scores * HEAD_DIM ** (-0.5)
    allowed = (key_pos[None, :] >= lowest[:, None]) & (key_pos[None, :] <= query_pos[:, None])
    scores = jnp.where(allowed, scores, -jnp.inf)
    largest = jnp.max(scores, axis=1, keepdims=True)
    powers = jnp.exp(scores - largest)
    totals = jnp.sum(powers, axis=1, keepdims=True)
    weights = powers.astype(jnp.bfloat16)
    context = jnp.dot(weights, value_tile, preferred_element_type=jnp.float32) / totals
    return context.astype(jnp.bfloat16)


def on_device(queries, key_rows, value_rows, w_out, first_key):
    place = lax.axis_index("blk")
    query_h, key_h, value_h = (
        lax.all_to_all(queries, "head", split_axis=1, concat_axis=0, tiled=True),
        lax.all_to_all(key_rows, "head", split_axis=1, concat_axis=0, tiled=True),
        lax.all_to_all(value_rows, "head", split_axis=1, concat_axis=0, tiled=True),
    )
    earlier = from_behind(jnp.stack((key_h, value_h)), "blk", 1)
    key_prev = earlier[0]
    value_prev = earlier[1]
    span_rows = query_h.shape[0]
    width = query_h.shape[1]
    local_heads = width // HEAD_DIM
    key_all = jnp.concatenate([key_prev, key_h], axis=0)
    value_all = jnp.concatenate([value_prev, value_h], axis=0)
    start = place * span_rows
    query_span = min(512, span_rows)
    spans = span_rows // query_span
    key_count = span_rows + query_span

    def one_tile(item):
        span_id = item // local_heads
        head_id = item % local_heads
        row_start = span_id * query_span
        column = head_id * HEAD_DIM
        query_tile = lax.dynamic_slice(query_h, (row_start, column), (query_span, HEAD_DIM))
        key_tile = lax.dynamic_slice(key_all, (row_start, column), (key_count, HEAD_DIM))
        value_tile = lax.dynamic_slice(value_all, (row_start, column), (key_count, HEAD_DIM))
        lowest = lax.dynamic_slice_in_dim(first_key, row_start, query_span)
        query_pos = start + row_start + jnp.arange(query_span, dtype=jnp.int32)
        key_pos = start - span_rows + row_start + jnp.arange(key_count, dtype=jnp.int32)
        return attend(query_tile, key_tile, value_tile, lowest, query_pos, key_pos)

    tiles = lax.map(one_tile, jnp.arange(spans * local_heads, dtype=jnp.int32))
    context = (
        tiles.reshape(spans, local_heads, query_span, HEAD_DIM)
        .transpose(0, 2, 1, 3)
        .reshape(span_rows, width)
    )
    regrouped = lax.all_to_all(context, "head", split_axis=0, concat_axis=1, tiled=True)
    summed = jnp.dot(
        regrouped,
        lax.all_gather(w_out, "head", axis=0, tiled=True),
        preferred_element_type=jnp.float32,
    )
    return summed.astype(jnp.bfloat16)


def solution(mesh):
    placed = (
        P(("blk", "head"), None),
        P(("blk", "head"), None),
        P(("blk", "head"), None),
        P("head", None),
        P("blk"),
    )
    return jax.shard_map(
        on_device, mesh=mesh, in_specs=placed, out_specs=P(("blk", "head"), None), check_vma=False
    )
```

profile of v0, /device:TPU:1, one launch (start us, length us, event | category | flops | bytes accessed | tf_op | source)
XLA Modules:
  0.0 209.6 jit_solution(6131552187451697892)
XLA Ops:
  7.6 0.9 copy_bitcast_fusion.1
  8.5 11.6 %all-to-all-start.1 = ((bf16[128,16,128]{2,0,1:T(8,128)(2,1)}), bf16[128,16,128]{2,0,1:T(8,128)(2,1)S(1)}, u32[]{:S(2)}, u32[]{:S(2)}) async-start(bf16[128,16,128]{2,0,1:T(8,128)(2,1)} %copy_bitcast_fusion.1), calls=%async_computation.1 | async-start | bytes 1048576 | tf_op jit(solution)/shard_map/all_to_all | solution.py:34
  20.1 1.2 copy_bitcast_fusion
  21.3 14.7 %all-to-all-done.1 = bf16[128,16,128]{2,0,1:T(8,128)(2,1)S(1)} async-done(((bf16[128,16,128]{2,0,1:T(8,128)(2,1)}), bf16[128,16,128]{2,0,1:T(8,128)(2,1)S(1)}, u32[]{:S(2)}, u32[]{:S(2)}) %all-to-all-start.1) | async-done | bytes 524320 | tf_op jit(solution)/shard_map/all_to_all | solution.py:34
  36.0 28.6 %all_to_all.76 = bf16[128,16,128]{2,0,1:T(8,128)(2,1)S(1)} all-to-all(bf16[128,16,128]{2,0,1:T(8,128)(2,1)S(1)} %copy_bitcast_fusion), channel_id=1, replica_groups=mesh['blk'=16,'head'=16] {'head'}, dimensions={1} | all-to-all | bytes 1048576 | tf_op jit(solution)/shard_map/all_to_all | solution.py:35
  64.6 1.2 pad_maximum_fusion
  65.7 7.4 %collective-permute-start = (bf16[2,2048,128]{2,1,0:T(8,128)(2,1)}, bf16[2,2048,128]{2,1,0:T(8,128)(2,1)S(1)}, u32[]{:S(2)}, u32[]{:S(2)}) collective-permute-start(bf16[2,2048,128]{2,1,0:T(8,128)(2,1)} %pad_maximum_fusion), channel_id=1, source_target_pairs={{0,16},{16,32},{32,48},{48,64},{64,80},{80,96},{96,112},{112,128},... | collective-permute-start | bytes 3145736 | tf_op jit(solution)/shard_map/ppermute | solution.py:12
  73.1 0.9 copy_bitcast_fusion.2
  74.1 3.7 %all-to-all-start = ((bf16[128,16,128]{2,0,1:T(8,128)(2,1)}), bf16[128,16,128]{2,0,1:T(8,128)(2,1)S(1)}, u32[]{:S(2)}, u32[]{:S(2)}) async-start(bf16[128,16,128]{2,0,1:T(8,128)(2,1)} %copy_bitcast_fusion.2), calls=%async_computation | async-start | bytes 1048576 | tf_op jit(solution)/shard_map/all_to_all | solution.py:33
  77.7 7.4 %collective-permute-done = bf16[2,2048,128]{2,1,0:T(8,128)(2,1)S(1)} collective-permute-done((bf16[2,2048,128]{2,1,0:T(8,128)(2,1)}, bf16[2,2048,128]{2,1,0:T(8,128)(2,1)S(1)}, u32[]{:S(2)}, u32[]{:S(2)}) %collective-permute-start) | collective-permute-done | bytes 1048608 | tf_op jit(solution)/shard_map/ppermute | solution.py:12
  85.2 1.2 pad_maximum_fusion.1
  86.4 13.1 %all-to-all-done = bf16[128,16,128]{2,0,1:T(8,128)(2,1)S(1)} async-done(((bf16[128,16,128]{2,0,1:T(8,128)(2,1)}), bf16[128,16,128]{2,0,1:T(8,128)(2,1)S(1)}, u32[]{:S(2)}, u32[]{:S(2)}) %all-to-all-start) | async-done | bytes 524320 | tf_op jit(solution)/shard_map/all_to_all | solution.py:33
  99.5 74.9 %while.12 = (s32[]{:T(128)}, bf16[8,512,64]{1,2,0:T(8,128)(2,1)}, s32[8]{0:T(128)S(1)}, s32[]{:T(128)}, s32[2048]{0:T(1024)}, /*index=5*/s32[]{:T(128)}, bf16[20...) while((s32[]{:T(128)}, bf16[8,512,64]{1,2,0:T(8,128)(2,1)}, ...), condition=%wide.region_3.4_spmd, body=%wide.region_0.3_spmd.sunk | while | flops 348719136 | bytes 17282060 | solution.py:63
  103.5 2.7 %fusion.33 = (f32[512]{0:T(512)S(1)}, f32[512,2560]{1,0:T(8,128)S(1)}) fusion(bf16[4096,128]{1,0:T(8,128)(2,1)} %get-tuple-element.243, s32[]{:T(128)S(6)} %select_n.55, s32[]{:T(128)S(6)} %select_n.57, bf16[2048,128]{1,0:T(8,128)(2,1)S(1)} %get-tuple-element.242, s32[]{:T(128)S(6)} %select_n.58, s32[512]{0:T(512)S(1)} %iota_add_fusion.4, ...), kind=kOutput, calls=%fused_computation.25.clone.1 | convolution fusion | flops 175635968 | bytes 6049792 | tf_op jit(solution)/shard_map/while/body/eval_jaxpr/dot_general | solution.py:16
  107.0 1.9 fusion.35
  112.8 2.7 %fusion.33 = (f32[512]{0:T(512)S(1)}, f32[512,2560]{1,0:T(8,128)S(1)}) fusion(bf16[4096,128]{1,0:T(8,128)(2,1)} %get-tuple-element.243, s32[]{:T(128)S(6)} %select_n.55, s32[]{:T(128)S(6)} %select_n.57, bf16[2048,128]{1,0:T(8,128)(2,1)S(1)} %get-tuple-element.242, s32[]{:T(128)S(6)} %select_n.58, s32[512]{0:T(512)S(1)} %iota_add_fusion.4, ...), kind=kOutput, calls=%fused_computation.25.clone.1 | convolution fusion | flops 175635968 | bytes 6049792 | tf_op jit(solution)/shard_map/while/body/eval_jaxpr/dot_general | solution.py:16
  116.3 1.9 fusion.35
  122.2 2.7 %fusion.33 = (f32[512]{0:T(512)S(1)}, f32[512,2560]{1,0:T(8,128)S(1)}) fusion(bf16[4096,128]{1,0:T(8,128)(2,1)} %get-tuple-element.243, s32[]{:T(128)S(6)} %select_n.55, s32[]{:T(128)S(6)} %select_n.57, bf16[2048,128]{1,0:T(8,128)(2,1)S(1)} %get-tuple-element.242, s32[]{:T(128)S(6)} %select_n.58, s32[512]{0:T(512)S(1)} %iota_add_fusion.4, ...), kind=kOutput, calls=%fused_computation.25.clone.1 | convolution fusion | flops 175635968 | bytes 6049792 | tf_op jit(solution)/shard_map/while/body/eval_jaxpr/dot_general | solution.py:16
  125.7 1.9 fusion.35
  131.5 2.7 %fusion.33 = (f32[512]{0:T(512)S(1)}, f32[512,2560]{1,0:T(8,128)S(1)}) fusion(bf16[4096,128]{1,0:T(8,128)(2,1)} %get-tuple-element.243, s32[]{:T(128)S(6)} %select_n.55, s32[]{:T(128)S(6)} %select_n.57, bf16[2048,128]{1,0:T(8,128)(2,1)S(1)} %get-tuple-element.242, s32[]{:T(128)S(6)} %select_n.58, s32[512]{0:T(512)S(1)} %iota_add_fusion.4, ...), kind=kOutput, calls=%fused_computation.25.clone.1 | convolution fusion | flops 175635968 | bytes 6049792 | tf_op jit(solution)/shard_map/while/body/eval_jaxpr/dot_general | solution.py:16
  135.0 1.9 fusion.35
  140.9 2.7 %fusion.33 = (f32[512]{0:T(512)S(1)}, f32[512,2560]{1,0:T(8,128)S(1)}) fusion(bf16[4096,128]{1,0:T(8,128)(2,1)} %get-tuple-element.243, s32[]{:T(128)S(6)} %select_n.55, s32[]{:T(128)S(6)} %select_n.57, bf16[2048,128]{1,0:T(8,128)(2,1)S(1)} %get-tuple-element.242, s32[]{:T(128)S(6)} %select_n.58, s32[512]{0:T(512)S(1)} %iota_add_fusion.4, ...), kind=kOutput, calls=%fused_computation.25.clone.1 | convolution fusion | flops 175635968 | bytes 6049792 | tf_op jit(solution)/shard_map/while/body/eval_jaxpr/dot_general | solution.py:16
  144.4 1.9 fusion.35
  150.3 2.7 %fusion.33 = (f32[512]{0:T(512)S(1)}, f32[512,2560]{1,0:T(8,128)S(1)}) fusion(bf16[4096,128]{1,0:T(8,128)(2,1)} %get-tuple-element.243, s32[]{:T(128)S(6)} %select_n.55, s32[]{:T(128)S(6)} %select_n.57, bf16[2048,128]{1,0:T(8,128)(2,1)S(1)} %get-tuple-element.242, s32[]{:T(128)S(6)} %select_n.58, s32[512]{0:T(512)S(1)} %iota_add_fusion.4, ...), kind=kOutput, calls=%fused_computation.25.clone.1 | convolution fusion | flops 175635968 | bytes 6049792 | tf_op jit(solution)/shard_map/while/body/eval_jaxpr/dot_general | solution.py:16
  153.8 1.9 fusion.35
  159.6 2.7 %fusion.33 = (f32[512]{0:T(512)S(1)}, f32[512,2560]{1,0:T(8,128)S(1)}) fusion(bf16[4096,128]{1,0:T(8,128)(2,1)} %get-tuple-element.243, s32[]{:T(128)S(6)} %select_n.55, s32[]{:T(128)S(6)} %select_n.57, bf16[2048,128]{1,0:T(8,128)(2,1)S(1)} %get-tuple-element.242, s32[]{:T(128)S(6)} %select_n.58, s32[512]{0:T(512)S(1)} %iota_add_fusion.4, ...), kind=kOutput, calls=%fused_computation.25.clone.1 | convolution fusion | flops 175635968 | bytes 6049792 | tf_op jit(solution)/shard_map/while/body/eval_jaxpr/dot_general | solution.py:16
  163.1 1.9 fusion.35
  169.0 2.7 %fusion.33 = (f32[512]{0:T(512)S(1)}, f32[512,2560]{1,0:T(8,128)S(1)}) fusion(bf16[4096,128]{1,0:T(8,128)(2,1)} %get-tuple-element.243, s32[]{:T(128)S(6)} %select_n.55, s32[]{:T(128)S(6)} %select_n.57, bf16[2048,128]{1,0:T(8,128)(2,1)S(1)} %get-tuple-element.242, s32[]{:T(128)S(6)} %select_n.58, s32[512]{0:T(512)S(1)} %iota_add_fusion.4, ...), kind=kOutput, calls=%fused_computation.25.clone.1 | convolution fusion | flops 175635968 | bytes 6049792 | tf_op jit(solution)/shard_map/while/body/eval_jaxpr/dot_general | solution.py:16
  172.5 1.9 fusion.35
  174.4 1.4 copy.26
  176.2 21.1 %all_to_all.77 = bf16[16,128,128]{1,2,0:T(8,128)(2,1)S(1)} all-to-all(bf16[16,128,128]{1,2,0:T(8,128)(2,1)S(1)} %copy.18), channel_id=1, replica_groups=mesh['blk'=16,'head'=16] {'head'}, dimensions={0} | all-to-all | bytes 1048576 | tf_op jit(solution)/shard_map/all_to_all | solution.py:69
  197.3 5.5 %convolution_convert_fusion = bf16[128,2048]{1,0:T(8,128)(2,1)} fusion(bf16[128,2048]{0,1:T(8,128)(2,1)S(1)} %bitcast.56, bf16[2048,2048]{1,0:T(8,128)(2,1)} %all-gather.2.cloned.1.call-done), kind=kOutput, calls=%fused_computation.15 | convolution fusion | flops 1074003968 | bytes 9437184 | tf_op jit(solution)/shard_map/dot_general | solution.py:70
  (52 shorter events, 19.5 us)
Async XLA Ops:
  6.5 1.0 copy-start
  6.5 66.6 %copy-start.1 = (bf16[128,2048]{1,0:T(8,128)(2,1)S(1)}, bf16[128,2048]{1,0:T(8,128)(2,1)}, u32[]{:S(2)}) copy-start(bf16[128,2048]{1,0:T(8,128)(2,1)} %param.7) | copy-start | bytes 1572868
  6.5 190.8 %all-gather.2.cloned.1.call-start = ((), (), s32[]{:S(2)}) async-start(), calls=%async_computation.4 | async-start | bytes 8912896 | tf_op jit(solution)/shard_map/all_gather | solution.py:72
  8.5 27.5 %all-to-all-start.1 = ((bf16[128,16,128]{2,0,1:T(8,128)(2,1)}), bf16[128,16,128]{2,0,1:T(8,128)(2,1)S(1)}, u32[]{:S(2)}, u32[]{:S(2)}) async-start(bf16[128,16,128]{2,0,1:T(8,128)(2,1)} %copy_bitcast_fusion.1), calls=%async_computation.1 | async-start | bytes 1048576 | tf_op jit(solution)/shard_map/all_to_all | solution.py:34
  65.7 19.5 %collective-permute-start = (bf16[2,2048,128]{2,1,0:T(8,128)(2,1)}, bf16[2,2048,128]{2,1,0:T(8,128)(2,1)S(1)}, u32[]{:S(2)}, u32[]{:S(2)}) collective-permute-start(bf16[2,2048,128]{2,1,0:T(8,128)(2,1)} %pad_maximum_fusion), channel_id=1, source_target_pairs={{0,16},{16,32},{32,48},{48,64},{64,80},{80,96},{96,112},{112,128},... | collective-permute-start | bytes 3145736 | tf_op jit(solution)/shard_map/ppermute | solution.py:12
  74.1 25.4 %all-to-all-start = ((bf16[128,16,128]{2,0,1:T(8,128)(2,1)}), bf16[128,16,128]{2,0,1:T(8,128)(2,1)S(1)}, u32[]{:S(2)}, u32[]{:S(2)}) async-start(bf16[128,16,128]{2,0,1:T(8,128)(2,1)} %copy_bitcast_fusion.2), calls=%async_computation | async-start | bytes 1048576 | tf_op jit(solution)/shard_map/all_to_all | solution.py:33
Sparse Core Ops, SparseCore 0:
  9.9 155.0 all-gather.1
where the time goes:
time: 211 us; the launch traced here: 210 us
  blocking collectives  49.7 us (24%)
  matrix products  42 us (20%)
  waiting for transfers between devices  35.9 us (17%)
  starting transfers between devices  22.6 us (11%)
  loops' own time  20.4 us (10%)
  local copies, waits for them, and re-layouts  16.4 us (8%)
  between operations  13.5 us (6%)
  other arithmetic  9.18 us (4%)
    all_to_all x1, blocking collectives, on_device(): lax.all_to_all(value_rows, 'head', split_axis=1, concat_axis=0, tiled=True)  28.6 us
    dot_general x8, matrix products, attend(): lax.dot_general(query_tile, key_tile, (((1,), (1,)), ((), ())), preferred...  21.3 us
    all_to_all x1, blocking collectives, on_device(): lax.all_to_all(context, 'head', split_axis=0, concat_axis=1, tiled=True)  21.1 us
    another operation x1, loops' own time, on_device(): tiles = lax.map(one_tile, jnp.arange(spans * local_heads, dtype=jnp.int32))  20.4 us
    dot_general x8, matrix products, attend(): jnp.dot(weights, value_tile, preferred_element_type=jnp.float32) / totals  15.2 us
    all_to_all x1, waiting for transfers between devices, on_device(): lax.all_to_all(key_rows, 'head', split_axis=1, concat_axis=0, tiled=True)  14.7 us
    all_to_all x1, waiting for transfers between devices, on_device(): lax.all_to_all(queries, 'head', split_axis=1, concat_axis=0, tiled=True)  13.1 us
    all_to_all x1, starting transfers between devices, on_device(): lax.all_to_all(key_rows, 'head', split_axis=1, concat_axis=0, tiled=True)  11.6 us
  transfers between devices with their start and end apart: 4, of which 3 were waited for; matrix products, arithmetic and copies ran while one was open for 29% of the time, Pallas kernels for 0%

commit v1 on v0

v1 whole, which is shorter than its diff:
```python
import functools
import math

import jax
import jax.numpy as jnp
from jax import lax
from jax.experimental import pallas as pl
from jax.experimental.pallas import tpu as pltpu
from jax.sharding import PartitionSpec as P


HEAD_DIM = 64
LANES = 128
TILE = 256
FACTOR = math.log2(math.e) * HEAD_DIM ** (-0.5)
DOT = (((1,), (1,)), ((), ()))


def scores(q, low, k_ref, s_ref, kbs, base, diag, largest):
    key_lane = lax.broadcasted_iota(jnp.int32, (TILE, TILE), 1)
    key_row = lax.broadcasted_iota(jnp.int32, (TILE, TILE), 0)
    for u, kb in enumerate(kbs):
        keys = k_ref[2 * kb : 2 * kb + 2].reshape(TILE, LANES)
        s = lax.dot_general(q, keys, DOT, preferred_element_type=jnp.float32)
        allowed = (key_lane + (base + kb * TILE)) >= low
        if kb == diag:
            allowed = allowed & (key_lane <= key_row)
        s = jnp.where(allowed, s, -jnp.inf)
        s_ref[u] = s
        top = jnp.maximum(s[:, :LANES], s[:, LANES:])
        largest = top if largest is None else jnp.maximum(largest, top)
    return jnp.max(largest, axis=1, keepdims=True)

def weigh(v_ref, s_ref, kbs, shift):
    total = acc = None
    for u, kb in enumerate(kbs):
        values = v_ref[2 * kb : 2 * kb + 2].reshape(TILE, LANES)
        p = jnp.exp2(s_ref[u] * FACTOR - shift)
        part = p[:, :LANES] + p[:, LANES:]
        total = part if total is None else total + part
        term = jnp.dot(p.astype(jnp.bfloat16), values, preferred_element_type=jnp.float32)
        acc = term if acc is None else acc + term
    return total, acc

def own_kernel(low0, low1, q0, q1, k_ref, v_ref, acc_o, m_o, l_o, s_ref):
    tiles = k_ref.shape[0] // 2
    lane = lax.broadcasted_iota(jnp.int32, (TILE, LANES), 1)
    for j in range(tiles // 2):
        @pl.when(pl.program_id(0) == j)
        def _():
            for slot, (low, q, tile) in enumerate(((low0, q0, j), (low1, q1, tiles - 1 - j))):
                kbs = range(tile + 1)
                low = jnp.concatenate([low[...]] * 2, axis=1)
                q = q[...].reshape(TILE, LANES)
                accs = []
                for head in range(2):
                    mine = (lane < HEAD_DIM) if head == 0 else (lane >= HEAD_DIM)
                    qh = jnp.where(mine, q, jnp.zeros_like(q))
                    top = scores(qh, low, k_ref, s_ref.at[slot, head], kbs, tiles * TILE, tile, None)
                    l, acc = weigh(v_ref, s_ref.at[slot, head], kbs, top * FACTOR)
                    m_o[slot, head] = jnp.broadcast_to(top, (TILE, LANES))
                    l_o[slot, head] = l
                    accs.append(acc)
                acc_o[slot] = jnp.where(lane < HEAD_DIM, accs[0], accs[1])

def prev_kernel(low0, low1, q0, q1, k_ref, v_ref, acc_i, m_i, l_i, o_ref, s_ref, *, head):
    tiles = k_ref.shape[0] // 2
    lane = lax.broadcasted_iota(jnp.int32, (TILE, LANES), 1)
    mine = (lane < HEAD_DIM) if head == 0 else (lane >= HEAD_DIM)
    half = lax.broadcasted_iota(jnp.int32, (HEAD_DIM, LANES), 1) < HEAD_DIM
    for j in range(tiles // 2):
        @pl.when(pl.program_id(0) == j)
        def _():
            for slot, (low, q, tile) in enumerate(((low0, q0, j), (low1, q1, tiles - 1 - j))):
                kbs = range(tile, tiles)
                low = jnp.concatenate([low[...]] * 2, axis=1)
                q = q[...].reshape(TILE, LANES)
                qh = jnp.where(mine, q, jnp.zeros_like(q))
                own = m_i[slot]
                top = scores(qh, low, k_ref, s_ref.at[slot, 0], kbs, 0, None, own)
                shift = top * FACTOR
                l, acc = weigh(v_ref, s_ref.at[slot, 0], kbs, shift)
                keep = jnp.exp2(own * FACTOR - shift)
                l = l + l_i[slot] * keep
                acc = acc + acc_i[slot] * keep
                out = acc / jnp.sum(l, axis=1, keepdims=True)
                for g in range(2):
                    lo = out[g * LANES : g * LANES + HEAD_DIM]
                    hi = out[g * LANES + HEAD_DIM : (g + 1) * LANES]
                    if head == 0:
                        packed = jnp.where(half, lo, pltpu.roll(hi, HEAD_DIM, 1))
                    else:
                        packed = jnp.where(half, pltpu.roll(lo, HEAD_DIM, 1), hi)
                    o_ref[2 * tile + g] = packed.astype(jnp.bfloat16)

def specs(tiles):
    last = tiles - 1
    return dict(
        low0=pl.BlockSpec((TILE, LANES), lambda j: (j, 0)),
        low1=pl.BlockSpec((TILE, LANES), lambda j: (last - j, 0)),
        q0=pl.BlockSpec((2, None, LANES, LANES), lambda j: (j, 0, 0, 0)),
        q1=pl.BlockSpec((2, None, LANES, LANES), lambda j: (last - j, 0, 0, 0)),
        k=pl.BlockSpec((2 * tiles, None, LANES, LANES), lambda j: (0, 0, 0, 0), pipeline_mode=pl.Buffered(1)),
        v=pl.BlockSpec((2 * tiles, None, LANES, LANES), lambda j: (0, 1, 0, 0), pipeline_mode=pl.Buffered(1)),
    )

def scratch(tiles):
    return [pltpu.VMEM((2, 2, tiles, TILE, TILE), jnp.float32)]

def cost(heads, tiles):
    n = heads * tiles * TILE * (tiles + 1) * TILE // 2
    return pl.CostEstimate(flops=4 * n * LANES, bytes_accessed=6 << 20, transcendentals=n)

def own_part(low, qw, kv):
    tiles = kv.shape[0] // 2
    sp = specs(tiles)
    f = jnp.float32
    return pl.pallas_call(
        own_kernel, grid=(tiles // 2,),
        in_specs=[sp[n] for n in ("low0", "low1", "q0", "q1", "k", "v")],
        out_shape=[jax.ShapeDtypeStruct((tiles, TILE, LANES), f), jax.ShapeDtypeStruct((tiles, 2, TILE, LANES), f), jax.ShapeDtypeStruct((tiles, 2, TILE, LANES), f)],
        out_specs=[pl.BlockSpec((2, TILE, LANES), lambda j: (j, 0, 0)), pl.BlockSpec((2, 2, TILE, LANES), lambda j: (j, 0, 0, 0)), pl.BlockSpec((2, 2, TILE, LANES), lambda j: (j, 0, 0, 0))],
        scratch_shapes=scratch(tiles),
        compiler_params=pltpu.CompilerParams(dimension_semantics=("arbitrary",), vmem_limit_bytes=60 << 20),
        cost_estimate=cost(2, tiles), name="own_part")(low, low, qw, qw, kv, kv)

def prev_part(low, qw, prev, state, head):
    tiles = prev.shape[0] // 2
    sp = specs(tiles)
    acc, m, l = state
    stat = pl.BlockSpec((2, None, TILE, LANES), lambda j: (j, head, 0, 0))
    return pl.pallas_call(
        functools.partial(prev_kernel, head=head), grid=(tiles // 2,),
        in_specs=[sp[n] for n in ("low0", "low1", "q0", "q1", "k", "v")] + [pl.BlockSpec((2, TILE, LANES), lambda j: (j, 0, 0)), stat, stat],
        out_shape=jax.ShapeDtypeStruct((2 * tiles, HEAD_DIM, LANES), jnp.bfloat16),
        out_specs=pl.BlockSpec((2 * tiles, HEAD_DIM, LANES), lambda j: (0, 0, 0)),
        scratch_shapes=scratch(tiles),
        compiler_params=pltpu.CompilerParams(dimension_semantics=("arbitrary",), vmem_limit_bytes=60 << 20),
        cost_estimate=cost(1, tiles))(low, low, qw, qw, prev, prev, acc, m, l)


def project_kernel(a_ref, b_ref, *refs):
    count = len(refs) - 3
    pieces, o_ref, held, sem = refs[:count], refs[count], refs[count + 1], refs[count + 2]
    for i in range(count):
        pltpu.make_async_copy(pieces[i], held.at[i], sem.at[i]).start()
    here = lax.axis_index("blk")
    core = lax.rem(here, 2)
    x, y = here // 8, lax.rem(here // 2, 4)
    half = lax.broadcasted_iota(jnp.int32, (HEAD_DIM, LANES), 1) < HEAD_DIM
    low, high = [], []
    for g in range(a_ref.shape[0]):
        a, b = a_ref[g].astype(jnp.float32), b_ref[g].astype(jnp.float32)
        low.append(jnp.where(half, a, pltpu.roll(b, HEAD_DIM, 1)))
        high.append(jnp.where(half, pltpu.roll(a, HEAD_DIM, 1), b))
    ctx = [jnp.concatenate(part, axis=1).astype(jnp.bfloat16) for part in (low, high)]
    ctx = jnp.concatenate(ctx, axis=0)

    def step(i, carry):
        for k in range(2):
            pltpu.make_async_copy(pieces[k], held.at[2 * i + k], sem.at[2 * i + k]).wait()
        turn = i // 2
        dx, dy = lax.rem(i, 2), turn + lax.rem(turn // 2, 2) * (5 - 2 * turn)
        pair = 4 * lax.rem(x + dx, 2) + lax.rem(y + 4 - dy, 4)
        w = jnp.concatenate([held[2 * i], held[2 * i + 1]], axis=1)
        out = jnp.dot(ctx, w, preferred_element_type=jnp.float32).astype(jnp.bfloat16)
        for part, where in ((0, core), (1, 1 - core)):
            at = pl.multiple_of((2 * pair + where) * LANES, LANES)
            o_ref[:, pl.ds(at, LANES)] = out[:, part * LANES : (part + 1) * LANES]
        return carry

    lax.fori_loop(0, count // 2, step, 0)


def project(a, b, pieces):
    rows = 2 * a.shape[1]
    depth = pieces[0].shape[0]
    width = len(pieces) * LANES
    return pl.pallas_call(
        project_kernel,
        out_shape=jax.ShapeDtypeStruct((rows, width), jnp.bfloat16),
        in_specs=[pl.BlockSpec(memory_space=pltpu.VMEM)] * 2
        + [pl.BlockSpec(memory_space=pl.ANY)] * len(pieces),
        out_specs=pl.BlockSpec(memory_space=pltpu.VMEM),
        scratch_shapes=[
            pltpu.VMEM((len(pieces), depth, LANES), jnp.bfloat16),
            pltpu.SemaphoreType.DMA((len(pieces),)),
        ],
        compiler_params=pltpu.CompilerParams(vmem_limit_bytes=60 << 20),
        cost_estimate=pl.CostEstimate(
            flops=2 * rows * depth * width, bytes_accessed=2 * depth * width, transcendentals=0
        ),
        name="project",
    )(a, b, *pieces)


def layer(queries, key_rows, value_rows, w_out, first_key):
    place = lax.axis_index("blk")
    blks = lax.axis_size("blk")
    heads = lax.axis_size("head")
    rows = queries.shape[0]
    span = heads * rows
    split = lambda x: x.reshape(rows, heads, LANES).transpose(1, 0, 2)

    column = lax.dynamic_slice(w_out, (0, place * LANES), (w_out.shape[0], LANES))
    column = jnp.broadcast_to(column[None], (heads,) + column.shape)
    qw = jnp.stack([split(queries), column], axis=1)
    qw = lax.all_to_all(qw, "head", 0, 0, tiled=True)
    kv = jnp.stack([split(key_rows), split(value_rows)], axis=1)
    kv = lax.all_to_all(kv, "head", 0, 0, tiled=True)
    prev = lax.ppermute(kv, "blk", [(i, i + 1) for i in range(blks - 1)])

    mine = qw[:, 1].reshape(heads * w_out.shape[0], LANES)
    far, _ = lax.optimization_barrier((mine, kv))
    pieces = []
    for dy in (0, 1, 3, 2):
        for dx in (0, 1):
            pairs = []
            for i in range(blks):
                x, y, core = i // 8, (i // 2) % 4, i % 2
                pairs.append((i, (x ^ dx) * 8 + ((y + dy) % 4) * 2 + core))
            if dx == dy == 0:
                piece = mine
            else:
                piece = lax.ppermute(far if dy == 2 else mine, "blk", pairs)
            other = lax.ppermute(piece, "blk", [(i, i ^ 1) for i in range(blks)])
            pieces += [piece, other]

    low = jnp.broadcast_to((first_key - (place * span - span))[:, None], (span, LANES))
    state = own_part(low, qw, kv)
    a = prev_part(low, qw, prev, state, 0)
    a = lax.all_to_all(a, "head", 0, 0, tiled=True)
    b = prev_part(low, qw, prev, state, 1)
    b = lax.all_to_all(b, "head", 0, 0, tiled=True)
    return project(a, b, pieces)


def solution(mesh):
    placed = (
        P(("blk", "head"), None),
        P(("blk", "head"), None),
        P(("blk", "head"), None),
        P("head", None),
        P("blk"),
    )
    return jax.shard_map(layer, mesh=mesh, in_specs=placed, out_specs=P(("blk", "head"), None), check_vma=False)
```

time: 211 us -> 210 us (level)
  the two profiles are of different devices: /device:TPU:1 before, /device:TPU:26 now
where the time goes in v1:
time: 210 us; the launch traced here: 209 us
  waiting for transfers between devices  102 us (49%)
  starting transfers between devices  62.3 us (30%)
  Pallas kernels  34.5 us (16%)
  local copies, waits for them, and re-layouts  7.91 us (4%)
  other arithmetic  2.15 us (1%)
    ppermute x7, waiting for transfers between devices, layer(): piece = lax.ppermute(far if dy == 2 else mine, 'blk', pairs)  33.1 us
    all_to_all x1, waiting for transfers between devices, layer(): kv = lax.all_to_all(kv, 'head', 0, 0, tiled=True)  28.8 us
    all_to_all x1, waiting for transfers between devices, layer(): qw = lax.all_to_all(qw, 'head', 0, 0, tiled=True)  25.4 us
    ppermute x8, starting transfers between devices, layer(): other = lax.ppermute(piece, 'blk', [(i, i ^ 1) for i in range(blks)])  18.1 us
    pallas_call x2, Pallas kernels, prev_part(): pl.pallas_call(functools.partial(prev_kernel, head=head), grid=(tiles //...  16.5 us
    all_to_all x1, starting transfers between devices, layer(): b = lax.all_to_all(b, 'head', 0, 0, tiled=True)  12.5 us
    pallas_call x1, Pallas kernels, own_part(): pl.pallas_call(own_kernel, grid=(tiles // 2,), in_specs=[sp[n] for n in (...  12.2 us
    all_to_all x1, waiting for transfers between devices, layer(): a = lax.all_to_all(a, 'head', 0, 0, tiled=True)  12 us
  transfers between devices with their start and end apart: 20, of which 6 were waited for; matrix products, arithmetic and copies ran while one was open for 2% of the time, Pallas kernels for 14%

profile of v1, /device:TPU:26, one launch (start us, length us, event | category | flops | bytes accessed | tf_op | source)
XLA Modules:
  0.0 209.2 jit_solution(367810629011370236)
XLA Ops:
  0.0 1.4 copy.6
  1.8 1.1 pad_maximum_fusion
  2.9 10.1 %all-to-all-start = ((bf16[16,2,128,128]{3,2,1,0:T(8,128)(2,1)}), bf16[16,2,128,128]{3,2,1,0:T(8,128)(2,1)S(1)}, u32[]{:S(2)}, u32[]{:S(2)}) async-start(bf16[16,2,128,128]{3,2,1,0:T(8,128)(2,1)} %pad_maximum_fusion), calls=%async_computation | async-start | bytes 2097152 | tf_op jit(solution)/shard_map/all_to_all | solution.py:208
  13.6 1.3 copy.10
  15.2 1.1 pad_maximum_fusion.1
  16.3 25.4 %all-to-all-done.q0.q1 = bf16[16,2,128,128]{3,2,1,0:T(8,128)(2,1)S(1)} async-done(((bf16[16,2,128,128]{3,2,1,0:T(8,128)(2,1)}), bf16[16,2,128,128]{3,2,1,0:T(8,128)(2,1)S(1)}, u32[]{:S(2)}, u32[]{:S(2)}) %all-to-all-start) | async-done | bytes 1048608 | tf_op jit(solution)/shard_map/all_to_all | solution.py:208
  41.7 4.4 %all-to-all-start.1 = ((bf16[16,2,128,128]{3,2,1,0:T(8,128)(2,1)}), bf16[16,2,128,128]{3,2,1,0:T(8,128)(2,1)S(1)}, u32[]{:S(2)}, u32[]{:S(2)}) async-start(bf16[16,2,128,128]{3,2,1,0:T(8,128)(2,1)} %pad_maximum_fusion.1), calls=%async_computation.1 | async-start | bytes 2097152 | tf_op jit(solution)/shard_map/all_to_all | solution.py:210
  46.1 28.8 %all-to-all-done.1.k_ref.v_ref = bf16[16,2,128,128]{3,2,1,0:T(8,128)(2,1)S(1)} async-done(((bf16[16,2,128,128]{3,2,1,0:T(8,128)(2,1)}), bf16[16,2,128,128]{3,2,1,0:T(8,128)(2,1)S(1)}, u32[]{:S(2)}, u32[]{:S(2)}) %all-to-all-start.1) | async-done | bytes 1048608 | tf_op jit(solution)/shard_map/all_to_all | solution.py:210
  74.8 1.0 copy-done.6
  75.8 1.2 collective-permute-start.12
  77.1 1.9 collective-permute-start
  79.0 3.3 %collective-permute-start.14 = (bf16[2048,128]{1,0:T(8,128)(2,1)S(1)}, bf16[2048,128]{1,0:T(8,128)(2,1)}, u32[]{:S(2)}, u32[]{:S(2)}) collective-permute-start(bf16[2048,128]{1,0:T(8,128)(2,1)S(1)} %bitcast.14), channel_id=1, source_target_pairs={{0,192},{16,208},{32,224},{48,240},{64,128},{80,144},{96,160},{112... | collective-permute-start | bytes 1572872 | tf_op jit(solution)/shard_map/ppermute | solution.py:225
  82.2 0.8 collective-permute-start.10
  83.0 0.9 collective-permute-start.2
  83.9 28.9 %collective-permute-done.12.refs_12_ = bf16[2048,128]{1,0:T(8,128)(2,1)S(1)} collective-permute-done((bf16[2048,128]{1,0:T(8,128)(2,1)S(1)}, bf16[2048,128]{1,0:T(8,128)(2,1)S(1)}, u32[]{:S(2)}, u32[]{:S(2)}) %collective-permute-start.12) | collective-permute-done | bytes 524320 | tf_op jit(solution)/shard_map/ppermute | solution.py:225
  112.8 0.8 copy-done.7
  113.6 2.0 collective-permute-start.6
  115.8 4.2 %collective-permute-done.2.refs_2_ = bf16[2048,128]{1,0:T(8,128)(2,1)} collective-permute-done((bf16[2048,128]{1,0:T(8,128)(2,1)S(1)}, bf16[2048,128]{1,0:T(8,128)(2,1)}, u32[]{:S(2)}, u32[]{:S(2)}) %collective-permute-start.2) | collective-permute-done | bytes 524320 | tf_op jit(solution)/shard_map/ppermute | solution.py:225
  120.0 16.4 %collective-permute-start.1 = (bf16[2048,128]{1,0:T(8,128)(2,1)S(1)}, bf16[2048,128]{1,0:T(8,128)(2,1)}, u32[]{:S(2)}, u32[]{:S(2)}) collective-permute-start(bf16[2048,128]{1,0:T(8,128)(2,1)S(1)} %bitcast.20), channel_id=1, source_target_pairs={{0,16},{16,0},{32,48},{48,32},{64,80},{80,64},{96,112},{112,96},{1... | collective-permute-start | bytes 1572872 | tf_op jit(solution)/shard_map/ppermute | solution.py:226
  136.4 0.5 collective-permute-start.15
  136.9 1.4 broadcast_in_dim.2.low0.low1
  138.3 12.2 %own_part.1 = (f32[8,256,128]{2,1,0:T(8,128)}, f32[8,2,256,128]{3,2,1,0:T(8,128)}, f32[8,2,256,128]{3,2,1,0:T(8,128)}) custom-call(s32[2048,128]{1,0:T(8,128)} %broadcast_in_dim.2.low0.low1, s32[2048,128]{1,0:T(8,128)} %broadcast_in_dim.2.low0.low1, bf16[16,2,128,128]{3,2,1,0:T(8,128)(2,1)} %copy-done.1, bf16[16,2,128,128]{3,2,1,0:T(8,128)(2,1)} %copy-done.1, ...), custom_call_target="tpu_custom_call" | custom-call | flops 2415919104 | bytes 6291456 | tf_op jit(solution)/shard_map/own_part/pallas_call | solution.py:118
  150.6 8.3 %shard_map.56 = bf16[16,64,128]{2,1,0:T(8,128)(2,1)} custom-call(s32[2048,128]{1,0:T(8,128)} %broadcast_in_dim.2.low0.low1, s32[2048,128]{1,0:T(8,128)} %broadcast_in_dim.2.low0.low1, bf16[16,2,128,128]{3,2,1,0:T(8,128)(2,1)} %copy-done.1, bf16[16,2,128,128]{3,2,1,0:T(8,128)(2,1)} %copy-done.1, bf16[16,2,128,128]{3,2,1,0:T(8,128)(2,1)} %copy-done.2, ...), custom_call_target="tpu_custom_call" | custom-call | flops 1207959552 | bytes 6291456 | tf_op jit(solution)/shard_map/pallas_call | solution.py:132
  158.8 12.5 %all-to-all-start.3 = ((bf16[16,64,128]{2,1,0:T(8,128)(2,1)}), bf16[16,64,128]{2,1,0:T(8,128)(2,1)S(1)}, u32[]{:S(2)}, u32[]{:S(2)}) async-start(bf16[16,64,128]{2,1,0:T(8,128)(2,1)} %shard_map.56), calls=%async_computation.3 | async-start | bytes 524288 | tf_op jit(solution)/shard_map/all_to_all | solution.py:234
  171.5 0.5 collective-permute-start.3
  172.1 0.4 collective-permute-start.7
  172.6 8.2 %shard_map.55 = bf16[16,64,128]{2,1,0:T(8,128)(2,1)} custom-call(s32[2048,128]{1,0:T(8,128)} %broadcast_in_dim.2.low0.low1, s32[2048,128]{1,0:T(8,128)} %broadcast_in_dim.2.low0.low1, bf16[16,2,128,128]{3,2,1,0:T(8,128)(2,1)} %copy-done.1, bf16[16,2,128,128]{3,2,1,0:T(8,128)(2,1)} %copy-done.1, bf16[16,2,128,128]{3,2,1,0:T(8,128)(2,1)} %copy-done.2, ...), custom_call_target="tpu_custom_call" | custom-call | flops 1207959552 | bytes 6291456 | tf_op jit(solution)/shard_map/pallas_call | solution.py:132
  180.8 2.6 %all-to-all-done.3.b_ref = bf16[16,64,128]{2,1,0:T(8,128)(2,1)S(1)} async-done(((bf16[16,64,128]{2,1,0:T(8,128)(2,1)}), bf16[16,64,128]{2,1,0:T(8,128)(2,1)S(1)}, u32[]{:S(2)}, u32[]{:S(2)}) %all-to-all-start.3) | async-done | bytes 262176 | tf_op jit(solution)/shard_map/all_to_all | solution.py:234
  183.4 7.0 %all-to-all-start.2 = ((bf16[16,64,128]{2,1,0:T(8,128)(2,1)}), bf16[16,64,128]{2,1,0:T(8,128)(2,1)S(1)}, u32[]{:S(2)}, u32[]{:S(2)}) async-start(bf16[16,64,128]{2,1,0:T(8,128)(2,1)} %shard_map.55), calls=%async_computation.2 | async-start | bytes 524288 | tf_op jit(solution)/shard_map/all_to_all | solution.py:232
  190.6 12.0 %all-to-all-done.2.a_ref = bf16[16,64,128]{2,1,0:T(8,128)(2,1)S(1)} async-done(((bf16[16,64,128]{2,1,0:T(8,128)(2,1)}), bf16[16,64,128]{2,1,0:T(8,128)(2,1)S(1)}, u32[]{:S(2)}, u32[]{:S(2)}) %all-to-all-start.2) | async-done | bytes 262176 | tf_op jit(solution)/shard_map/all_to_all | solution.py:232
  202.6 0.7 copy-done.5
  203.3 5.7 %project.1 = bf16[128,2048]{1,0:T(8,128)(2,1)} custom-call(bf16[16,64,128]{2,1,0:T(8,128)(2,1)} %copy-done.5, bf16[16,64,128]{2,1,0:T(8,128)(2,1)} %copy-done.4, bf16[2048,128]{1,0:T(8,128)(2,1)} %bitcast.21, bf16[2048,128]{1,0:T(8,128)(2,1)} %collective-permute-done.1.refs_1_, bf16[2048,128]{1,0:T(8,128)(2,1)} %collective-permute-done.2.refs_2_, ...), custom_call_target="tpu_custom_call" | custom-call | flops 1073741824 | bytes 8388608 | tf_op jit(solution)/shard_map/project/pallas_call | solution.py:179
  (53 shorter events, 1.9 us)
Async XLA Ops:
  0.0 1.7 copy-start
  1.8 11.2 %copy-start.12 = (bf16[128,2048]{1,0:T(8,128)(2,1)S(1)}, bf16[128,2048]{1,0:T(8,128)(2,1)}, u32[]{:S(2)}) copy-start(bf16[128,2048]{1,0:T(8,128)(2,1)} %param.6) | copy-start | bytes 1572868
  2.9 38.8 %all-to-all-start = ((bf16[16,2,128,128]{3,2,1,0:T(8,128)(2,1)}), bf16[16,2,128,128]{3,2,1,0:T(8,128)(2,1)S(1)}, u32[]{:S(2)}, u32[]{:S(2)}) async-start(bf16[16,2,128,128]{3,2,1,0:T(8,128)(2,1)} %pad_maximum_fusion), calls=%async_computation | async-start | bytes 2097152 | tf_op jit(solution)/shard_map/all_to_all | solution.py:208
  16.3 97.3 %copy-start.13 = (s32[2048]{0:T(1024)S(1)}, s32[2048]{0:T(1024)}, u32[]{:S(2)}) copy-start(s32[2048]{0:T(1024)} %param.9) | copy-start | bytes 24580
  41.7 96.6 %copy-start.1 = (bf16[16,2,128,128]{3,2,1,0:T(8,128)(2,1)}, bf16[16,2,128,128]{3,2,1,0:T(8,128)(2,1)S(1)}, u32[]{:S(2)}) copy-start(bf16[16,2,128,128]{3,2,1,0:T(8,128)(2,1)S(1)} %all-to-all-done.q0.q1) | copy-start | bytes 3145732
  41.7 33.2 %all-to-all-start.1 = ((bf16[16,2,128,128]{3,2,1,0:T(8,128)(2,1)}), bf16[16,2,128,128]{3,2,1,0:T(8,128)(2,1)S(1)}, u32[]{:S(2)}, u32[]{:S(2)}) async-start(bf16[16,2,128,128]{3,2,1,0:T(8,128)(2,1)} %pad_maximum_fusion.1), calls=%async_computation.1 | async-start | bytes 2097152 | tf_op jit(solution)/shard_map/all_to_all | solution.py:210
  46.1 104.5 %copy-start.3 = (bf16[16,1,128,128]{3,2,1,0:T(8,128)(2,1)}, bf16[16,1,128,128]{3,2,1,0:T(8,128)(2,1)S(1)}, u32[]{:S(2)}) copy-start(bf16[16,1,128,128]{3,2,1,0:T(8,128)(2,1)S(1)} %slice.4) | copy-start | bytes 1572868
  74.8 1.0 copy-start.6
  75.8 36.9 %collective-permute-start.12 = (bf16[2048,128]{1,0:T(8,128)(2,1)S(1)}, bf16[2048,128]{1,0:T(8,128)(2,1)S(1)}, u32[]{:S(2)}, u32[]{:S(2)}) collective-permute-start(bf16[2048,128]{1,0:T(8,128)(2,1)S(1)} %bitcast.13), channel_id=1, source_target_pairs={{0,64},{16,80},{32,96},{48,112},{64,0},{80,16},{96,32},{112,48},{1... | collective-permute-start | bytes 1572872 | tf_op jit(solution)/shard_map/ppermute | solution.py:225
  77.1 59.3 %collective-permute-start = (bf16[16,2,128,128]{3,2,1,0:T(8,128)(2,1)}, bf16[16,2,128,128]{3,2,1,0:T(8,128)(2,1)S(1)}, u32[]{:S(2)}, u32[]{:S(2)}) collective-permute-start(bf16[16,2,128,128]{3,2,1,0:T(8,128)(2,1)} %copy-done.6), channel_id=1, source_target_pairs={{0,16},{16,32},{32,48},{48,64},{64,80},{80,96},{96,112},{112,128},... | collective-permute-start | bytes 3145736 | tf_op jit(solution)/shard_map/ppermute | solution.py:211
  79.0 34.6 %collective-permute-start.14 = (bf16[2048,128]{1,0:T(8,128)(2,1)S(1)}, bf16[2048,128]{1,0:T(8,128)(2,1)}, u32[]{:S(2)}, u32[]{:S(2)}) collective-permute-start(bf16[2048,128]{1,0:T(8,128)(2,1)S(1)} %bitcast.14), channel_id=1, source_target_pairs={{0,192},{16,208},{32,224},{48,240},{64,128},{80,144},{96,160},{112... | collective-permute-start | bytes 1572872 | tf_op jit(solution)/shard_map/ppermute | solution.py:225
  82.2 33.3 %collective-permute-start.10 = (bf16[2048,128]{1,0:T(8,128)(2,1)S(1)}, bf16[2048,128]{1,0:T(8,128)(2,1)}, u32[]{:S(2)}, u32[]{:S(2)}) collective-permute-start(bf16[2048,128]{1,0:T(8,128)(2,1)S(1)} %bitcast.15), channel_id=1, source_target_pairs={{0,224},{16,240},{32,128},{48,144},{64,160},{80,176},{96,192},{112... | collective-permute-start | bytes 1572872 | tf_op jit(solution)/shard_map/ppermute | solution.py:225
  83.0 37.0 %collective-permute-start.2 = (bf16[2048,128]{1,0:T(8,128)(2,1)S(1)}, bf16[2048,128]{1,0:T(8,128)(2,1)}, u32[]{:S(2)}, u32[]{:S(2)}) collective-permute-start(bf16[2048,128]{1,0:T(8,128)(2,1)S(1)} %bitcast.16), channel_id=1, source_target_pairs={{0,128},{16,144},{32,160},{48,176},{64,192},{80,208},{96,224},{112... | collective-permute-start | bytes 1572872 | tf_op jit(solution)/shard_map/ppermute | solution.py:225
  113.6 22.8 %collective-permute-start.4 = (bf16[2048,128]{1,0:T(8,128)(2,1)S(1)}, bf16[2048,128]{1,0:T(8,128)(2,1)}, u32[]{:S(2)}, u32[]{:S(2)}) collective-permute-start(bf16[2048,128]{1,0:T(8,128)(2,1)S(1)} %bitcast.17), channel_id=1, source_target_pairs={{0,32},{16,48},{32,64},{48,80},{64,96},{80,112},{96,0},{112,16},{1... | collective-permute-start | bytes 1572872 | tf_op jit(solution)/shard_map/ppermute | solution.py:225
  113.6 57.8 %collective-permute-start.6 = (bf16[2048,128]{1,0:T(8,128)(2,1)S(1)}, bf16[2048,128]{1,0:T(8,128)(2,1)}, u32[]{:S(2)}, u32[]{:S(2)}) collective-permute-start(bf16[2048,128]{1,0:T(8,128)(2,1)S(1)} %bitcast.18), channel_id=1, source_target_pairs={{0,160},{16,176},{32,192},{48,208},{64,224},{80,240},{96,128},{112... | collective-permute-start | bytes 1572872 | tf_op jit(solution)/shard_map/ppermute | solution.py:225
  115.5 55.9 %collective-permute-start.8 = (bf16[2048,128]{1,0:T(8,128)(2,1)S(1)}, bf16[2048,128]{1,0:T(8,128)(2,1)}, u32[]{:S(2)}, u32[]{:S(2)}) collective-permute-start(bf16[2048,128]{1,0:T(8,128)(2,1)S(1)} %bitcast.19), channel_id=1, source_target_pairs={{0,96},{16,112},{32,0},{48,16},{64,32},{80,48},{96,64},{112,80},{1... | collective-permute-start | bytes 1572872 | tf_op jit(solution)/shard_map/ppermute | solution.py:225
  120.0 52.0 %collective-permute-start.1 = (bf16[2048,128]{1,0:T(8,128)(2,1)S(1)}, bf16[2048,128]{1,0:T(8,128)(2,1)}, u32[]{:S(2)}, u32[]{:S(2)}) collective-permute-start(bf16[2048,128]{1,0:T(8,128)(2,1)S(1)} %bitcast.20), channel_id=1, source_target_pairs={{0,16},{16,0},{32,48},{48,32},{64,80},{80,64},{96,112},{112,96},{1... | collective-permute-start | bytes 1572872 | tf_op jit(solution)/shard_map/ppermute | solution.py:226
  136.4 35.7 %collective-permute-start.13 = (bf16[2048,128]{1,0:T(8,128)(2,1)}, bf16[2048,128]{1,0:T(8,128)(2,1)}, u32[]{:S(2)}, u32[]{:S(2)}) collective-permute-start(bf16[2048,128]{1,0:T(8,128)(2,1)} %copy-done.7), channel_id=1, source_target_pairs={{0,16},{16,0},{32,48},{48,32},{64,80},{80,64},{96,112},{112,96},{1... | collective-permute-start | bytes 1572872 | tf_op jit(solution)/shard_map/ppermute | solution.py:226
  136.4 14.2 %copy-start.2 = (bf16[16,2,128,128]{3,2,1,0:T(8,128)(2,1)}, bf16[16,2,128,128]{3,2,1,0:T(8,128)(2,1)S(1)}, u32[]{:S(2)}) copy-start(bf16[16,2,128,128]{3,2,1,0:T(8,128)(2,1)S(1)} %collective-permute-done.k_ref.v_ref) | copy-start | bytes 3145732
  136.4 36.1 %collective-permute-start.15 = (bf16[2048,128]{1,0:T(8,128)(2,1)}, bf16[2048,128]{1,0:T(8,128)(2,1)}, u32[]{:S(2)}, u32[]{:S(2)}) collective-permute-start(bf16[2048,128]{1,0:T(8,128)(2,1)} %collective-permute-done.14.refs_14_), channel_id=1, source_target_pairs={{0,16},{16,0},{32,48},{48,32},{64,80},{80,64},{96,112},{112,96},{1... | collective-permute-start | bytes 1572872 | tf_op jit(solution)/shard_map/ppermute | solution.py:226
  158.8 24.6 %all-to-all-start.3 = ((bf16[16,64,128]{2,1,0:T(8,128)(2,1)}), bf16[16,64,128]{2,1,0:T(8,128)(2,1)S(1)}, u32[]{:S(2)}, u32[]{:S(2)}) async-start(bf16[16,64,128]{2,1,0:T(8,128)(2,1)} %shard_map.56), calls=%async_computation.3 | async-start | bytes 524288 | tf_op jit(solution)/shard_map/all_to_all | solution.py:234
  171.4 19.1 %collective-permute-start.11 = (bf16[2048,128]{1,0:T(8,128)(2,1)}, bf16[2048,128]{1,0:T(8,128)(2,1)S(1)}, u32[]{:S(2)}, u32[]{:S(2)}) collective-permute-start(bf16[2048,128]{1,0:T(8,128)(2,1)} %collective-permute-done.10.refs_10_), channel_id=1, source_target_pairs={{0,16},{16,0},{32,48},{48,32},{64,80},{80,64},{96,112},{112,96},{1... | collective-permute-start | bytes 1572872 | tf_op jit(solution)/shard_map/ppermute | solution.py:226
  171.5 19.0 %collective-permute-start.3 = (bf16[2048,128]{1,0:T(8,128)(2,1)}, bf16[2048,128]{1,0:T(8,128)(2,1)S(1)}, u32[]{:S(2)}, u32[]{:S(2)}) collective-permute-start(bf16[2048,128]{1,0:T(8,128)(2,1)} %collective-permute-done.2.refs_2_), channel_id=1, source_target_pairs={{0,16},{16,0},{32,48},{48,32},{64,80},{80,64},{96,112},{112,96},{1... | collective-permute-start | bytes 1572872 | tf_op jit(solution)/shard_map/ppermute | solution.py:226
  172.0 18.5 %collective-permute-start.5 = (bf16[2048,128]{1,0:T(8,128)(2,1)}, bf16[2048,128]{1,0:T(8,128)(2,1)S(1)}, u32[]{:S(2)}, u32[]{:S(2)}) collective-permute-start(bf16[2048,128]{1,0:T(8,128)(2,1)} %collective-permute-done.4.refs_4_), channel_id=1, source_target_pairs={{0,16},{16,0},{32,48},{48,32},{64,80},{80,64},{96,112},{112,96},{1... | collective-permute-start | bytes 1572872 | tf_op jit(solution)/shard_map/ppermute | solution.py:226
  172.1 18.5 %collective-permute-start.7 = (bf16[2048,128]{1,0:T(8,128)(2,1)}, bf16[2048,128]{1,0:T(8,128)(2,1)S(1)}, u32[]{:S(2)}, u32[]{:S(2)}) collective-permute-start(bf16[2048,128]{1,0:T(8,128)(2,1)} %collective-permute-done.6.refs_6_), channel_id=1, source_target_pairs={{0,16},{16,0},{32,48},{48,32},{64,80},{80,64},{96,112},{112,96},{1... | collective-permute-start | bytes 1572872 | tf_op jit(solution)/shard_map/ppermute | solution.py:226
  172.5 18.1 %collective-permute-start.9 = (bf16[2048,128]{1,0:T(8,128)(2,1)}, bf16[2048,128]{1,0:T(8,128)(2,1)}, u32[]{:S(2)}, u32[]{:S(2)}) collective-permute-start(bf16[2048,128]{1,0:T(8,128)(2,1)} %collective-permute-done.8.refs_8_), channel_id=1, source_target_pairs={{0,16},{16,0},{32,48},{48,32},{64,80},{80,64},{96,112},{112,96},{1... | collective-permute-start | bytes 1572872 | tf_op jit(solution)/shard_map/ppermute | solution.py:226
  183.4 19.1 %copy-start.4 = (bf16[16,64,128]{2,1,0:T(8,128)(2,1)}, bf16[16,64,128]{2,1,0:T(8,128)(2,1)S(1)}, u32[]{:S(2)}) copy-start(bf16[16,64,128]{2,1,0:T(8,128)(2,1)S(1)} %all-to-all-done.3.b_ref) | copy-start | bytes 786436
  183.4 19.1 %all-to-all-start.2 = ((bf16[16,64,128]{2,1,0:T(8,128)(2,1)}), bf16[16,64,128]{2,1,0:T(8,128)(2,1)S(1)}, u32[]{:S(2)}, u32[]{:S(2)}) async-start(bf16[16,64,128]{2,1,0:T(8,128)(2,1)} %shard_map.55), calls=%async_computation.2 | async-start | bytes 524288 | tf_op jit(solution)/shard_map/all_to_all | solution.py:232
  190.5 12.1 %copy-start.8 = (bf16[2048,128]{1,0:T(8,128)(2,1)}, bf16[2048,128]{1,0:T(8,128)(2,1)S(1)}, u32[]{:S(2)}) copy-start(bf16[2048,128]{1,0:T(8,128)(2,1)S(1)} %collective-permute-done.11.refs_11_) | copy-start | bytes 1572868
  190.5 12.0 %copy-start.9 = (bf16[2048,128]{1,0:T(8,128)(2,1)}, bf16[2048,128]{1,0:T(8,128)(2,1)S(1)}, u32[]{:S(2)}) copy-start(bf16[2048,128]{1,0:T(8,128)(2,1)S(1)} %collective-permute-done.3.refs_3_) | copy-start | bytes 1572868
  190.5 12.0 %copy-start.10 = (bf16[2048,128]{1,0:T(8,128)(2,1)}, bf16[2048,128]{1,0:T(8,128)(2,1)S(1)}, u32[]{:S(2)}) copy-start(bf16[2048,128]{1,0:T(8,128)(2,1)S(1)} %collective-permute-done.5.refs_5_) | copy-start | bytes 1572868
  190.6 12.0 %copy-start.11 = (bf16[2048,128]{1,0:T(8,128)(2,1)}, bf16[2048,128]{1,0:T(8,128)(2,1)S(1)}, u32[]{:S(2)}) copy-start(bf16[2048,128]{1,0:T(8,128)(2,1)S(1)} %collective-permute-done.7.refs_7_) | copy-start | bytes 1572868
  (2 other events, 1.5 us)
